TPU v7x, 128 devices: a whole 4x4x4 slice. The times are simulated.
128 devices in a mesh: dp: 16 (over x, y), tensor: 8 (over z, core).
Axes of the slice: x: 4, y: 4, z: 4, core: 2. Of those that a mesh axis runs over, the one named last changes fastest.
Arguments:
- hidden_rows: bfloat16 [256, 32, 8192], P('tensor', 'dp'), may hold values from -6 to 6
- norm_gain: float32 [8192], replicated, may hold values from 0.1 to 1.9
- w_query: bfloat16 [8192, 4096], P(None, 'tensor'), may hold values from -0.0625 to 0.0625
- w_key: bfloat16 [8192, 1024], P(None, 'tensor'), may hold values from -0.0625 to 0.0625
- w_value: bfloat16 [8192, 1024], P(None, 'tensor'), may hold values from -0.0625 to 0.0625
- w_out: bfloat16 [4096, 8192], P('tensor'), may hold values from -1.5 to 1.5
- cache_keys: bfloat16 [32, 2048, 1024], P('dp', None, 'tensor'), may hold values from -6 to 6
- cache_values: bfloat16 [32, 2048, 1024], P('dp', None, 'tensor'), may hold values from -6 to 6
- slot_of_request: int32 [32], replicated, may hold values from 0 to 31, as said below
- span_length: int32 [32], replicated, may hold values from 1 to 256, as said below
- prefix_length: int32 [32], replicated, may hold values from 1 to 2048, as said below
Outputs:
- attention_out: bfloat16 [256, 32, 8192], P('tensor', 'dp')
Inputs may be any that keep to these rules, and one draw needn't show every extreme that they name: `slot_of_request`: a permutation of the slots 0 to 31; slot i lies on dp index i // 2, request r starts on dp index r // 2; there are 2 distinct numbers m, one of them 1, the same for every dp index, such that the 2 requests of dp index i have their slots on the dp indices i XOR m, one on each. `span_length`: some request uses all 256 new positions. `prefix_length`: some request has all 2048 cached positions.
All inputs are finite; a program needn't handle non-finite values.
Results may differ from a plain program's by a relative error of at most 0.019.
Values may be sent and summed in bfloat16 or wider, within the bound.
A program may use at most 128 MiB of HBM per device.

v0:
```python
import jax
import jax.numpy as jnp
from jax import lax
from jax.sharding import PartitionSpec as P

HD = 128
rope_base = 500000.0
norm_eps = 1e-05
masked = -1e30


def rotate(values, position):
    head_width = values.shape[-1]
    half_width = head_width // 2
    frequency = rope_base ** (-(jnp.arange(half_width, dtype=jnp.float32) * 2.0 / head_width))
    angles = position[..., None, None] * frequency
    cosine = jnp.cos(angles)
    sine_part = jnp.sin(angles)
    front_half = values[..., :half_width]
    back_half = values[..., half_width:]
    return jnp.concatenate(
        [front_half * cosine - back_half * sine_part, back_half * cosine + front_half * sine_part],
        axis=-1,
    )


def normalize(hidden_rows, norm_gain):
    floats = hidden_rows.astype(jnp.float32)
    return (
        floats * lax.rsqrt(jnp.mean(floats * floats, axis=-1, keepdims=True) + norm_eps) * norm_gain
    ).astype(jnp.bfloat16)


def project_group(normed, prefix_here, w_query, w_key, w_value):
    piece_rows = lax.all_gather(normed, "tensor", axis=0, tiled=True)
    row_count = piece_rows.shape[0]
    request_count = piece_rows.shape[1]
    positions = (prefix_here[None, :] + jnp.arange(row_count, dtype=jnp.int32)[:, None]).astype(
        jnp.float32
    )
    queries = jnp.einsum("nsd,df->nsf", piece_rows, w_query, preferred_element_type=jnp.float32)
    queries = rotate(queries.reshape(row_count, request_count, -1, HD), positions)
    keys_new = jnp.einsum("nsd,df->nsf", piece_rows, w_key, preferred_element_type=jnp.float32)
    keys_new = rotate(keys_new.reshape(row_count, request_count, -1, HD), positions)
    values_new = jnp.einsum("nsd,df->nsf", piece_rows, w_value, preferred_element_type=jnp.float32)
    return jnp.concatenate(
        [
            queries.reshape(row_count, request_count, -1).astype(jnp.bfloat16),
            keys_new.reshape(row_count, request_count, -1).astype(jnp.bfloat16),
            values_new.astype(jnp.bfloat16),
        ],
        axis=-1,
    )


def attend_slots(packed, cache_keys, cache_values, slot_prefix, slot_length, q_width, kv_width):
    span_rows = packed.shape[0]
    slot_count = packed.shape[1]
    kv_heads = kv_width // HD
    groups = q_width // kv_width
    prefix = cache_keys.shape[1]
    score_scale = HD ** (-0.5)
    queries = packed[..., :q_width].reshape(span_rows, slot_count, kv_heads, groups, HD)
    keys_new = packed[..., q_width : q_width + kv_width].reshape(
        span_rows, slot_count, kv_heads, HD
    )
    values_new = packed[..., q_width + kv_width :].reshape(span_rows, slot_count, kv_heads, HD)
    keys_old = cache_keys.reshape(slot_count, prefix, kv_heads, HD)
    values_old = cache_values.reshape(slot_count, prefix, kv_heads, HD)
    score_old = (
        jnp.einsum("csgmd,spgd->sgmcp", queries, keys_old, preferred_element_type=jnp.float32)
        * score_scale
    )
    score_new = (
        jnp.einsum("csgmd,jsgd->sgmcj", queries, keys_new, preferred_element_type=jnp.float32)
        * score_scale
    )
    keep_old = jnp.arange(prefix, dtype=jnp.int32)[None, :] < slot_prefix[:, None]
    row_index = jnp.arange(span_rows, dtype=jnp.int32)
    keep_new = (row_index[None, None, :] < slot_length[:, None, None]) & (
        row_index[None, None, :] <= row_index[None, :, None]
    )
    score_old = jnp.where(keep_old[:, None, None, None, :], score_old, masked)
    score_new = jnp.where(keep_new[:, None, None, :, :], score_new, masked)
    exp_old = jnp.exp(score_old)
    exp_new = jnp.exp(score_new)
    denominator = jnp.sum(exp_old, axis=-1, keepdims=True) + jnp.sum(
        exp_new, axis=-1, keepdims=True
    )
    weight_old = (exp_old / denominator).astype(jnp.bfloat16)
    weight_new = (exp_new / denominator).astype(jnp.bfloat16)
    mixed = jnp.einsum(
        "sgmcp,spgd->csgmd", weight_old, values_old, preferred_element_type=jnp.float32
    )
    mixed = mixed + jnp.einsum(
        "sgmcj,jsgd->csgmd", weight_new, values_new, preferred_element_type=jnp.float32
    )
    return mixed.astype(jnp.bfloat16).reshape(span_rows, slot_count, q_width)


def local(
    hidden_rows,
    norm_gain,
    w_query,
    w_key,
    w_value,
    w_out,
    cache_keys,
    cache_values,
    slot_of_request,
    span_length,
    prefix_length,
):
    data_size = lax.axis_size("dp")
    data_index = lax.axis_index("dp")
    per_device = hidden_rows.shape[1]
    q_width = w_query.shape[1]
    kv_width = w_key.shape[1]
    all_requests = slot_of_request.shape[0]
    request_ids = jnp.arange(all_requests, dtype=jnp.int32)
    devices = jnp.arange(data_size, dtype=jnp.int32)
    first_request = data_index * per_device
    my_slots = lax.dynamic_slice_in_dim(slot_of_request, first_request, per_device)
    send_table = (devices[:, None] == my_slots[None, :] // per_device).astype(jnp.bfloat16)
    slot_match = (
        slot_of_request[None, :]
        == (first_request + jnp.arange(per_device, dtype=jnp.int32))[:, None]
    )
    source_match = request_ids[None, :] // per_device == devices[:, None]
    recv_table = jnp.any(slot_match[:, None, :] & source_match[None, :, :], axis=-1).astype(
        jnp.bfloat16
    )
    slot_prefix = jnp.sum(jnp.where(slot_match, prefix_length[None, :], 0), axis=1)
    slot_length = jnp.sum(jnp.where(slot_match, span_length[None, :], 0), axis=1)
    normed = normalize(hidden_rows, norm_gain)
    outgoing = jnp.einsum(
        "js,csf->jcf", send_table, normed, preferred_element_type=jnp.float32
    ).astype(jnp.bfloat16)
    incoming = lax.all_to_all(outgoing, "dp", split_axis=0, concat_axis=0, tiled=True)
    slot_rows = jnp.einsum(
        "sj,jcf->csf", recv_table, incoming, preferred_element_type=jnp.float32
    ).astype(jnp.bfloat16)
    packed = project_group(slot_rows, slot_prefix, w_query, w_key, w_value)
    mixed = attend_slots(
        packed, cache_keys, cache_values, slot_prefix, slot_length, q_width, kv_width
    )
    outgoing_back = jnp.einsum(
        "sj,csf->jcf", recv_table, mixed, preferred_element_type=jnp.float32
    ).astype(jnp.bfloat16)
    returned = lax.all_to_all(outgoing_back, "dp", split_axis=0, concat_axis=0, tiled=True)
    request_heads = jnp.einsum(
        "js,jcf->csf", send_table, returned, preferred_element_type=jnp.float32
    ).astype(jnp.bfloat16)
    span_rows = request_heads.shape[0]
    flat_heads = request_heads.reshape(span_rows * per_device, q_width)
    summed = lax.psum_scatter(
        jnp.dot(flat_heads, w_out, preferred_element_type=jnp.float32).astype(jnp.bfloat16),
        "tensor",
        scatter_dimension=0,
        tiled=True,
    ).astype(jnp.float32)
    return summed.reshape(hidden_rows.shape[0], per_device, -1).astype(jnp.bfloat16)


def solution(mesh):
    placed = (
        P("tensor", "dp", None),
        P(),
        P(None, "tensor"),
        P(None, "tensor"),
        P(None, "tensor"),
        P("tensor", None),
        P("dp", None, "tensor"),
        P("dp", None, "tensor"),
        P(),
        P(),
        P(),
    )
    return jax.shard_map(
        local, mesh=mesh, in_specs=placed, out_specs=P("tensor", "dp", None), check_vma=False
    )
```

profile of v0, /device:TPU:1, one launch (start us, length us, event | category | flops | bytes accessed | tf_op | source)
XLA Modules:
  0.0 441.6 jit_solution(15629852325169047121)
XLA Ops:
  6.5 0.0 copy-start
  6.5 2.6 fusion.16
  9.1 0.7 and_select_fusion
  9.8 7.6 %convolution_convert_fusion.1 = bf16[16,32,8192]{2,0,1:T(8,128)(2,1)} fusion(bf16[32,2,8192]{2,1,0:T(2,128)(2,1)} %param.11, f32[8192]{0:T(1024)} %param.12, f32[32,2]{1,0:T(8,128)S(1)} %add_rsqrt_fusion, s32[2]{0:T(128)S(1)} %and_select_fusion), kind=kOutput, calls=%fused_computation.6 | convolution fusion | flops 23068704 | bytes 9470216 | tf_op jit(solution)/shard_map/js,csf->jcf/dot_general | solution.py:136
  17.5 11.2 %copy.63 = bf16[16,32,8192]{2,1,0:T(8,128)(2,1)} copy(bf16[16,32,8192]{2,0,1:T(8,128)(2,1)} %convolution_convert_fusion.1) | data formatting | bytes 16777216 | tf_op jit(solution)/shard_map/convert_element_type | solution.py:138
  28.7 7.8 %all-to-all-start = ((bf16[16,32,8192]{2,1,0:T(8,128)(2,1)}), bf16[16,32,8192]{2,1,0:T(8,128)(2,1)}, u32[]{:S(2)}, u32[]{:S(2)}) async-start(bf16[16,32,8192]{2,1,0:T(8,128)(2,1)} %copy.63), calls=%async_computation | async-start | bytes 16777216 | tf_op jit(solution)/shard_map/all_to_all | solution.py:139
  36.4 0.2 all-gather.2.cloned.1.call-start
  36.7 0.0 copy-done.4
  36.7 0.0 copy-done.5
  36.7 0.0 copy-done.6
  36.7 0.2 select_reduce_fusion
  36.9 0.1 and_reduce_fusion
  37.0 145.5 %all-to-all-done = bf16[16,32,8192]{2,1,0:T(8,128)(2,1)} async-done(((bf16[16,32,8192]{2,1,0:T(8,128)(2,1)}), bf16[16,32,8192]{2,1,0:T(8,128)(2,1)}, u32[]{:S(2)}, u32[]{:S(2)}) %all-to-all-start) | async-done | bytes 8388640 | tf_op jit(solution)/shard_map/all_to_all | solution.py:139
  182.5 9.4 %fusion.3 = bf16[32,2,8192]{2,1,0:T(2,128)(2,1)} fusion(bf16[16,32,8192]{2,1,0:T(8,128)(2,1)} %all-to-all-done, pred[2,16]{1,0:T(4,128)(4,1)S(1)} %and_reduce_fusion), kind=kOutput, calls=%fused_computation.8 | convolution fusion | flops 17301504 | bytes 9437216 | tf_op jit(solution)/shard_map/sj,jcf->csf/dot_general | solution.py:140
  191.9 0.0 all-gather.2.cloned.1.call-update
  191.9 0.3 reduce-scatter.2.cloned.1.call-start
  192.3 0.1 iota_compare_fusion.3
  192.3 0.1 add_convert_fusion.1
  192.4 0.1 broadcast_and_fusion
  192.5 1.7 multiply_cosine_fusion
  194.3 0.1 iota_compare_fusion.1
  194.4 53.7 %all-gather.2.cloned.1.call-done = bf16[256,2,8192]{2,1,0:T(2,128)(2,1)} async-done(((bf16[32,2,8192]{2,1,0:T(2,128)(2,1)}), bf16[256,2,8192]{2,1,0:T(2,128)(2,1)}) %all-gather.2.cloned.1.call-update) | async-done | bytes 8388624 | tf_op jit(solution)/shard_map/all_gather | solution.py:35
  248.0 8.9 %fusion.38 = f32[256,2,1,128]{0,3,1,2:T(8,128)S(1)} fusion(bf16[8192,128]{1,0:T(8,128)(2,1)} %param.14, bf16[256,2,8192]{2,1,0:T(2,128)(2,1)} %all-gather.2.cloned.1.call-done), kind=kOutput, calls=%fused_computation.38 | convolution fusion | flops 1073741824 | bytes 10747904 | tf_op jit(solution)/shard_map/nsd,df->nsf/dot_general | solution.py:43
  256.9 1.2 fusion.78
  258.1 0.0 copy-done.7
  258.1 13.0 %fusion.6 = f32[256,2,512]{2,0,1:T(8,128)} fusion(bf16[8192,512]{1,0:T(8,128)(2,1)} %param.13, bf16[256,2,8192]{2,1,0:T(2,128)(2,1)S(1)} %copy-done.7), kind=kOutput, calls=%fused_computation.11 | convolution fusion | flops 4294967296 | bytes 17825792 | tf_op jit(solution)/shard_map/nsd,df->nsf/dot_general | solution.py:41
  271.1 1.6 reshape.282
  272.7 0.6 fusion.91
  273.3 1.2 subtract_convert_fusion
  274.5 0.0 copy-start.2
  274.5 0.0 copy-start.3
  274.5 9.1 %fusion.2 = (f32[2,4,256]{2,1,0:T(4,128)S(1)}, f32[2,256,4,2048]{3,1,2,0:T(8,128)}) fusion(pred[2,2048]{1,0:T(4,128)(4,1)S(1)} %iota_compare_fusion.1, bf16[2,2048,128]{2,1,0:T(8,128)(2,1)} %param.17, bf16[256,2,4,64]{3,0,2,1:T(8,128)(2,1)S(1)} %get-tuple-element.9, bf16[256,2,4,64]{3,0,2,1:T(8,128)(2,1)S(1)} %get-tuple-element.8), kind=kOutput, calls=%fused_computation.4 | convolution fusion | flops 1087371264 | bytes 18362368 | tf_op jit(solution)/shard_map/csgmd,spgd->sgmcp/dot_general | solution.py:71
  283.6 0.0 copy-done.3
  283.6 2.1 fusion.22
  285.8 0.0 copy-start.8
  285.8 14.5 %fusion.57 = f32[2,128,4,256]{3,1,2,0:T(8,128)} fusion(f32[2,256,256,4]{2,1,3,0:T(8,128)} %get-tuple-element.19, f32[2,4,256]{2,1,0:T(4,128)S(1)} %add.80, pred[2,256,256]{1,2,0:T(8,128)(4,1)S(1)} %broadcast_and_fusion, bf16[8192,128]{1,0:T(8,128)(2,1)S(1)} %copy-done, bf16[256,2,8192]{2,1,0:T(2,128)(2,1)} %all-gather.2.cloned.1.call-done), kind=kOutput, calls=%fused_computation.44 | convolution fusion | flops 1210122240 | bytes 13770752 | tf_op jit(solution)/shard_map/sgmcj,jsgd->csgmd/dot_general | solution.py:95
  300.3 8.0 %fusion.32 = bf16[2,128,4,256]{3,1,2,0:T(8,128)(2,1)S(1)} fusion(f32[2,128,4,256]{3,1,2,0:T(8,128)} %fusion.57, f32[2,4,256]{2,1,0:T(4,128)S(1)} %add.80, f32[2,256,4,2048]{3,1,2,0:T(8,128)} %get-tuple-element.17, pred[2,2048]{1,0:T(4,128)(4,1)S(1)} %iota_compare_fusion.1, bf16[2,2048,128]{2,1,0:T(8,128)(2,1)S(1)} %copy-done.8), kind=kOutput, calls=%fused_computation.36 | convolution fusion | flops 1091043328 | bytes 19410944 | tf_op jit(solution)/shard_map/sgmcp,spgd->csgmd/dot_general | solution.py:92
  308.3 0.5 copy.75
  308.8 1.6 convolution_convert_fusion.3
  310.5 2.4 copy.76
  312.9 56.0 %all_to_all.10 = bf16[16,256,512]{2,1,0:T(8,128)(2,1)S(1)} all-to-all(bf16[16,256,512]{2,1,0:T(8,128)(2,1)S(1)} %copy.76), channel_id=1, replica_groups=mesh['dp'=16,'tensor'=8] {'dp'}, dimensions={0} | all-to-all | bytes 8388608 | tf_op jit(solution)/shard_map/all_to_all | solution.py:150
  368.8 2.5 fusion.35
  371.4 0.2 reshape.287
  371.6 0.0 copy-start.1
  371.6 10.2 %convolution_convert_fusion = bf16[512,8192]{1,0:T(8,128)(2,1)} fusion(bf16[512,512]{1,0:T(8,128)(2,1)S(1)} %reshape.287, bf16[512,8192]{1,0:T(8,128)(2,1)} %param.16), kind=kOutput, calls=%fused_computation.5 | convolution fusion | flops 4299161600 | bytes 17301504 | tf_op jit(solution)/shard_map/dot_general | solution.py:157
  381.8 0.0 reduce-scatter.2.cloned.1.call-update
  381.8 50.2 %reduce-scatter.2.cloned.1.call-done = bf16[64,8192]{1,0:T(8,128)(2,1)} async-done(((bf16[512,8192]{1,0:T(8,128)(2,1)}), bf16[64,8192]{1,0:T(8,128)(2,1)}) %reduce-scatter.2.cloned.1.call-update) | async-done | bytes 1048592 | tf_op jit(solution)/shard_map/reduce_scatter | solution.py:156
  432.1 2.5 convert_element_type.82
  (15 shorter events, 0.1 us)
Async XLA Ops:
  6.5 279.2 %copy-start = (bf16[8192,128]{1,0:T(8,128)(2,1)S(1)}, bf16[8192,128]{1,0:T(8,128)(2,1)}, u32[]{:S(2)}) copy-start(bf16[8192,128]{1,0:T(8,128)(2,1)} %param.15) | copy-start | bytes 6291460
  28.6 8.0 %copy-start.4 = (s32[32]{0:T(128)S(1)}, s32[32]{0:T(128)}, u32[]{:S(2)}) copy-start(s32[32]{0:T(128)} %param.19) | copy-start | bytes 388
  28.7 8.0 %copy-start.5 = (s32[32]{0:T(128)S(1)}, s32[32]{0:T(128)}, u32[]{:S(2)}) copy-start(s32[32]{0:T(128)} %param.20) | copy-start | bytes 388
  28.7 8.1 %copy-start.6 = (s32[32]{0:T(128)S(1)}, s32[32]{0:T(128)}, u32[]{:S(2)}) copy-start(s32[32]{0:T(128)} %param.21) | copy-start | bytes 388
  28.7 153.8 %all-to-all-start = ((bf16[16,32,8192]{2,1,0:T(8,128)(2,1)}), bf16[16,32,8192]{2,1,0:T(8,128)(2,1)}, u32[]{:S(2)}, u32[]{:S(2)}) async-start(bf16[16,32,8192]{2,1,0:T(8,128)(2,1)} %copy.63), calls=%async_computation | async-start | bytes 16777216 | tf_op jit(solution)/shard_map/all_to_all | solution.py:139
  36.4 211.6 %all-gather.2.cloned.1.call-start = ((), (), s32[]{:S(2)}) async-start(), calls=%async_computation.3 | async-start | bytes 9437184 | tf_op jit(solution)/shard_map/all_gather | solution.py:35
  191.9 240.1 %reduce-scatter.2.cloned.1.call-start = ((), (), s32[]{:S(2)}) async-start(), calls=%async_computation.4 | async-start | bytes 9437184 | tf_op jit(solution)/shard_map/reduce_scatter | solution.py:156
  248.0 10.1 %copy-start.7 = (bf16[256,2,8192]{2,1,0:T(2,128)(2,1)S(1)}, bf16[256,2,8192]{2,1,0:T(2,128)(2,1)}, u32[]{:S(2)}) copy-start(bf16[256,2,8192]{2,1,0:T(2,128)(2,1)} %all-gather.2.cloned.1.call-done) | copy-start | bytes 25165828
  274.5 9.1 %copy-start.2 = (bf16[256,2,64]{0,2,1:T(8,128)(2,1)S(1)}, bf16[256,2,64]{0,2,1:T(8,128)(2,1)}, u32[]{:S(2)}) copy-start(bf16[256,2,64]{0,2,1:T(8,128)(2,1)} %get-tuple-element.12) | copy-start | bytes 196612
  274.5 9.1 %copy-start.3 = (bf16[256,2,64]{0,2,1:T(8,128)(2,1)S(1)}, bf16[256,2,64]{0,2,1:T(8,128)(2,1)}, u32[]{:S(2)}) copy-start(bf16[256,2,64]{0,2,1:T(8,128)(2,1)} %get-tuple-element.13) | copy-start | bytes 196612
  285.8 14.5 %copy-start.8 = (bf16[2,2048,128]{2,1,0:T(8,128)(2,1)S(1)}, bf16[2,2048,128]{2,1,0:T(8,128)(2,1)}, u32[]{:S(2)}) copy-start(bf16[2,2048,128]{2,1,0:T(8,128)(2,1)} %param.18) | copy-start | bytes 3145732
  371.6 63.0 %copy-start.1 = (bf16[8192,128]{1,0:T(8,128)(2,1)S(1)}, bf16[8192,128]{1,0:T(8,128)(2,1)}, u32[]{:S(2)}) copy-start(bf16[8192,128]{1,0:T(8,128)(2,1)} %param.15) | copy-start | bytes 6291460
Sparse Core Ops, SparseCore 0:
  192.1 55.9 all-gather.1
  382.0 50.0 reduce-scatter.1
where the time goes:
time: 448 us; the launch traced here: 442 us
  waiting for transfers between devices  249 us (56%)
  matrix products  87 us (19%)
  blocking collectives  56 us (12%)
  local copies, waits for them, and re-layouts  19 us (4%)
  between operations  13.8 us (3%)
  starting transfers between devices  8.23 us (2%)
  other arithmetic  8.21 us (2%)
    all_to_all x1, waiting for transfers between devices, local(): lax.all_to_all(outgoing, 'dp', split_axis=0, concat_axis=0, tiled=True)  145 us
    all_to_all x1, blocking collectives, local(): lax.all_to_all(outgoing_back, 'dp', split_axis=0, concat_axis=0, tiled=True)  56 us
    all_gather x1, waiting for transfers between devices, project_group(): piece_rows = lax.all_gather(normed, 'tensor', axis=0, tiled=True)  53.7 us
    reduce_scatter x1, waiting for transfers between devices, local(): lax.psum_scatter(jnp.dot(flat_heads, w_out, preferred_element_type=jnp.fl...  50.2 us
    dot_general x1, matrix products, attend_slots(): jnp.einsum('sgmcj,jsgd->csgmd', weight_new, values_new, preferred_element...  14.5 us
    dot_general x1, matrix products, project_group(): jnp.einsum('nsd,df->nsf', piece_rows, w_query, preferred_element_type=jnp...  13 us
    convert_element_type x1, local copies, waits for them, and re-layouts, local(): outgoing = jnp.einsum('js,csf->jcf', send_table, normed, preferred_elemen...  11.2 us
    dot_general x1, matrix products, local(): jnp.dot(flat_heads, w_out, preferred_element_type=jnp.float32)  10.2 us
  transfers between devices with their start and end apart: 3, of which 3 were waited for; matrix products, arithmetic and copies ran while one was open for 1% of the time, Pallas kernels for 0%

commit v1 on v0

--- a/solution.py
+++ b/solution.py
@@ -32,7 +32,8 @@
 
 
 def project_group(normed, prefix_here, w_query, w_key, w_value):
-    piece_rows = lax.all_gather(normed, "tensor", axis=0, tiled=True)
+    sent = jnp.stack([normed] * lax.axis_size("tensor"))
+    piece_rows = jnp.concatenate(lax.all_to_all(sent, "tensor", 0, 0), axis=0)
     row_count = piece_rows.shape[0]
     request_count = piece_rows.shape[1]
     positions = (prefix_here[None, :] + jnp.arange(row_count, dtype=jnp.int32)[:, None]).astype(

time: 448 us -> 488 us (1.089)
  waiting for transfers between devices: 249 us -> 277 us
  local copies, waits for them, and re-layouts: 19 us -> 40.7 us
  matrix products: 87 us -> 70.2 us
  starting transfers between devices: 8.23 us -> 16.1 us
    all_to_all x0 -> x1, waiting for transfers between devices: none -> 81.4 us  [project_group(): piece_rows = jnp.concatenate(lax.all_to_all(sent, 'tensor', 0, 0), axis=0)]
    all_gather x1 -> x0, waiting for transfers between devices: 53.7 us -> none  [project_group(): piece_rows = lax.all_gather(normed, 'tensor', axis=0, tiled=True)]
    dot_general x0 -> x1, local copies, waits for them, and re-layouts: none -> 11.3 us  [project_group(): jnp.einsum('nsd,df->nsf', piece_rows, w_query, preferred_element_type=jnp...]
    all_to_all x0 -> x1, local copies, waits for them, and re-layouts: none -> 7.74 us  [project_group(): piece_rows = jnp.concatenate(lax.all_to_all(sent, 'tensor', 0, 0), axis=0)]
    all_to_all x0 -> x1, starting transfers between devices: none -> 7.64 us  [project_group(): piece_rows = jnp.concatenate(lax.all_to_all(sent, 'tensor', 0, 0), axis=0)]
    dot_general x1, matrix products: 14.5 us -> 7.89 us  [attend_slots(): jnp.einsum('sgmcj,jsgd->csgmd', weight_new, values_new, preferred_element...]
    dot_general x1, matrix products: 13 us -> 7.04 us  [project_group(): jnp.einsum('nsd,df->nsf', piece_rows, w_query, preferred_element_type=jnp...]
  transfers between devices with their start and end apart: 3 -> 3, of which waited for: 3 -> 3; matrix products, arithmetic and copies ran while one was open for 1% -> 3% of each run, Pallas kernels for 0% -> 0%
where the time goes in v1:
time: 488 us; the launch traced here: 481 us
  waiting for transfers between devices  277 us (57%)
  matrix products  70.2 us (14%)
  blocking collectives  58.1 us (12%)
  local copies, waits for them, and re-layouts  40.7 us (8%)
  starting transfers between devices  16.1 us (3%)
  between operations  13.8 us (3%)
  other arithmetic  5.29 us (1%)
    all_to_all x1, waiting for transfers between devices, local(): lax.all_to_all(outgoing, 'dp', split_axis=0, concat_axis=0, tiled=True)  146 us
    all_to_all x1, waiting for transfers between devices, project_group(): piece_rows = jnp.concatenate(lax.all_to_all(sent, 'tensor', 0, 0), axis=0)  81.4 us
    all_to_all x1, blocking collectives, local(): lax.all_to_all(outgoing_back, 'dp', split_axis=0, concat_axis=0, tiled=True)  58.1 us
    reduce_scatter x1, waiting for transfers between devices, local(): lax.psum_scatter(jnp.dot(flat_heads, w_out, preferred_element_type=jnp.fl...  49.8 us
    dot_general x1, local copies, waits for them, and re-layouts, project_group(): jnp.einsum('nsd,df->nsf', piece_rows, w_query, preferred_element_type=jnp...  11.3 us
    convert_element_type x1, local copies, waits for them, and re-layouts, local(): outgoing = jnp.einsum('js,csf->jcf', send_table, normed, preferred_elemen...  11.2 us
    dot_general x1, matrix products, local(): jnp.dot(flat_heads, w_out, preferred_element_type=jnp.float32)  10.2 us
  transfers between devices with their start and end apart: 3, of which 3 were waited for; matrix products, arithmetic and copies ran while one was open for 3% of the time, Pallas kernels for 0%

profile of v1, /device:TPU:1, one launch (start us, length us, event | category | flops | bytes accessed | tf_op | source)
XLA Modules:
  0.0 481.1 jit_solution(15073457416843971495)
XLA Ops:
  6.5 0.0 copy-start
  6.5 2.6 fusion.9
  9.1 0.7 and_select_fusion
  9.8 7.7 %convolution_convert_fusion.1 = bf16[16,32,8192]{2,0,1:T(8,128)(2,1)} fusion(bf16[32,2,8192]{2,1,0:T(2,128)(2,1)} %param.11, f32[8192]{0:T(1024)} %param.12, f32[32,2]{1,0:T(8,128)S(1)} %add_rsqrt_fusion, s32[2]{0:T(128)S(1)} %and_select_fusion), kind=kOutput, calls=%fused_computation.6 | convolution fusion | flops 23068704 | bytes 9470216 | tf_op jit(solution)/shard_map/js,csf->jcf/dot_general | solution.py:137
  17.5 11.2 %copy.64 = bf16[16,32,8192]{2,1,0:T(8,128)(2,1)} copy(bf16[16,32,8192]{2,0,1:T(8,128)(2,1)} %convolution_convert_fusion.1) | data formatting | bytes 16777216 | tf_op jit(solution)/shard_map/convert_element_type | solution.py:139
  28.7 8.2 %all-to-all-start = ((bf16[16,32,8192]{2,1,0:T(8,128)(2,1)}), bf16[16,32,8192]{2,1,0:T(8,128)(2,1)}, u32[]{:S(2)}, u32[]{:S(2)}) async-start(bf16[16,32,8192]{2,1,0:T(8,128)(2,1)} %copy.64), calls=%async_computation | async-start | bytes 16777216 | tf_op jit(solution)/shard_map/all_to_all | solution.py:140
  37.0 0.0 copy-done.4
  37.0 0.0 copy-done.5
  37.0 0.0 copy-done.6
  37.1 0.2 select_reduce_fusion
  37.2 0.1 and_reduce_fusion
  37.4 145.7 %all-to-all-done = bf16[16,32,8192]{2,1,0:T(8,128)(2,1)} async-done(((bf16[16,32,8192]{2,1,0:T(8,128)(2,1)}), bf16[16,32,8192]{2,1,0:T(8,128)(2,1)}, u32[]{:S(2)}, u32[]{:S(2)}) %all-to-all-start) | async-done | bytes 8388640 | tf_op jit(solution)/shard_map/all_to_all | solution.py:140
  183.1 8.5 %fusion.3 = bf16[32,2,8192]{2,1,0:T(2,128)(2,1)S(1)} fusion(bf16[16,32,8192]{2,1,0:T(8,128)(2,1)} %all-to-all-done, pred[2,16]{1,0:T(4,128)(4,1)S(1)} %and_reduce_fusion), kind=kOutput, calls=%fused_computation.8 | convolution fusion | flops 17301504 | bytes 9437216 | tf_op jit(solution)/shard_map/sj,jcf->csf/dot_general | solution.py:141
  191.5 0.6 copy.66
  192.1 4.2 stack.2
  196.4 7.6 %all-to-all-start.1 = ((bf16[8,32,2,8192]{3,1,2,0:T(8,128)(2,1)}), bf16[8,32,2,8192]{3,1,2,0:T(8,128)(2,1)}, u32[]{:S(2)}, u32[]{:S(2)}) async-start(bf16[8,32,2,8192]{3,1,2,0:T(8,128)(2,1)} %stack.2), calls=%async_computation.1 | async-start | bytes 16777216 | tf_op jit(solution)/shard_map/all_to_all | solution.py:36
  204.0 0.2 reduce-scatter.2.cloned.1.call-start
  204.2 11.3 %copy.88 = bf16[512,8192]{1,0:T(8,128)(2,1)} copy(bf16[512,8192]{0,1:T(8,128)(2,1)} %bitcast.150) | data formatting | bytes 16777216 | tf_op jit(solution)/shard_map/nsd,df->nsf/dot_general | solution.py:42
  215.5 0.1 iota_compare_fusion.3
  215.6 0.1 add_convert_fusion.1
  215.7 0.1 broadcast_and_fusion
  215.8 0.5 multiply_cosine_fusion.1
  216.4 0.1 iota_compare_fusion.1
  216.4 81.4 %all-to-all-done.1 = bf16[8,32,2,8192]{3,1,2,0:T(8,128)(2,1)} async-done(((bf16[8,32,2,8192]{3,1,2,0:T(8,128)(2,1)}), bf16[8,32,2,8192]{3,1,2,0:T(8,128)(2,1)}, u32[]{:S(2)}, u32[]{:S(2)}) %all-to-all-start.1) | async-done | bytes 8388640 | tf_op jit(solution)/shard_map/all_to_all | solution.py:36
  297.8 7.7 %copy.67 = bf16[8,32,2,8192]{3,1,0,2:T(8,128)(2,1)} copy(bf16[8,32,2,8192]{3,1,2,0:T(8,128)(2,1)} %all-to-all-done.1) | data formatting | bytes 16777216 | tf_op jit(solution)/shard_map/all_to_all | solution.py:36
  305.6 0.0 copy-done.3
  305.6 6.5 %fusion.33 = f32[256,2,1,128]{0,3,1,2:T(8,128)S(1)} fusion(bf16[256,2,8192]{2,0,1:T(8,128)(2,1)} %bitcast.147, bf16[8192,128]{1,0:T(8,128)(2,1)S(1)} %copy-done.3), kind=kOutput, calls=%fused_computation.33 | convolution fusion | flops 1073741824 | bytes 10747904 | tf_op jit(solution)/shard_map/nsd,df->nsf/dot_general | solution.py:44
  312.0 0.6 fusion.65
  312.6 0.0 copy-done.2
  312.6 0.0 copy-start.7
  312.6 7.0 %fusion.78 = f32[256,2,4,128]{0,3,2,1:T(8,128)S(1)} fusion(bf16[256,2,8192,1]{2,0,3,1:T(8,128)(2,1)S(1)} %bitcast.149, bf16[4,128,8192,1]{2,1,0,3:T(8,128)(2,1)} %bitcast.151), kind=kOutput, calls=%fused_computation.99 | convolution fusion | flops 4294967296 | bytes 17825792 | tf_op jit(solution)/shard_map/nsd,df->nsf/dot_general | solution.py:42
  319.7 0.2 subtract_convert_fusion
  319.9 0.0 copy-done.7
  319.9 7.7 %fusion.2 = (f32[2,4,256]{2,1,0:T(4,128)S(1)}, f32[2,256,4,2048]{3,1,2,0:T(8,128)}) fusion(pred[2,2048]{1,0:T(4,128)(4,1)S(1)} %iota_compare_fusion.1, bf16[2,2048,128]{2,1,0:T(8,128)(2,1)S(1)} %copy-done.7, bf16[256,2,4,64]{0,3,2,1:T(8,128)(2,1)S(1)} %get-tuple-element.9, bf16[256,2,4,64]{0,3,2,1:T(8,128)(2,1)S(1)} %get-tuple-element.8), kind=kOutput, calls=%fused_computation.4 | convolution fusion | flops 1087371264 | bytes 18362368 | tf_op jit(solution)/shard_map/csgmd,spgd->sgmcp/dot_general | solution.py:72
  327.6 2.0 fusion.17
  329.6 7.9 %fusion.46 = f32[2,128,4,256]{3,1,2,0:T(8,128)} fusion(f32[2,256,256,4]{2,1,3,0:T(8,128)} %get-tuple-element.17, f32[2,4,256]{2,1,0:T(4,128)S(1)} %add.80, pred[2,256,256]{1,2,0:T(8,128)(4,1)S(1)} %broadcast_and_fusion, bf16[256,2,8192]{2,0,1:T(8,128)(2,1)} %bitcast.148, bf16[8192,128]{1,0:T(8,128)(2,1)S(1)} %copy-done), kind=kOutput, calls=%fused_computation.39 | convolution fusion | flops 1210122240 | bytes 13770752 | tf_op jit(solution)/shard_map/sgmcj,jsgd->csgmd/dot_general | solution.py:96
  337.5 8.6 %fusion.27 = bf16[2,128,4,256]{3,1,2,0:T(8,128)(2,1)S(1)} fusion(f32[2,128,4,256]{3,1,2,0:T(8,128)} %fusion.46, f32[2,4,256]{2,1,0:T(4,128)S(1)} %add.80, f32[2,256,4,2048]{3,1,2,0:T(8,128)} %get-tuple-element.15, pred[2,2048]{1,0:T(4,128)(4,1)S(1)} %iota_compare_fusion.1, bf16[2,2048,128]{2,1,0:T(8,128)(2,1)} %param.18), kind=kOutput, calls=%fused_computation.31 | convolution fusion | flops 1091043328 | bytes 19410944 | tf_op jit(solution)/shard_map/sgmcp,spgd->csgmd/dot_general | solution.py:93
  346.0 0.5 copy.76
  346.6 1.6 convolution_convert_fusion.3
  348.2 2.4 copy.77
  350.6 58.1 %all_to_all.15 = bf16[16,256,512]{2,1,0:T(8,128)(2,1)S(1)} all-to-all(bf16[16,256,512]{2,1,0:T(8,128)(2,1)S(1)} %copy.77), channel_id=1, replica_groups=mesh['dp'=16,'tensor'=8] {'dp'}, dimensions={0} | all-to-all | bytes 8388608 | tf_op jit(solution)/shard_map/all_to_all | solution.py:151
  408.7 2.5 fusion.30
  411.3 0.2 reshape.291
  411.5 0.0 copy-start.1
  411.5 10.2 %convolution_convert_fusion = bf16[512,8192]{1,0:T(8,128)(2,1)} fusion(bf16[512,512]{1,0:T(8,128)(2,1)S(1)} %reshape.291, bf16[512,8192]{1,0:T(8,128)(2,1)} %param.16), kind=kOutput, calls=%fused_computation.5 | convolution fusion | flops 4299161600 | bytes 17301504 | tf_op jit(solution)/shard_map/dot_general | solution.py:158
  421.7 0.0 reduce-scatter.2.cloned.1.call-update
  421.7 49.8 %reduce-scatter.2.cloned.1.call-done = bf16[64,8192]{1,0:T(8,128)(2,1)} async-done(((bf16[512,8192]{1,0:T(8,128)(2,1)}), bf16[64,8192]{1,0:T(8,128)(2,1)}) %reduce-scatter.2.cloned.1.call-update) | async-done | bytes 1048592 | tf_op jit(solution)/shard_map/reduce_scatter | solution.py:157
  471.5 2.5 convert_element_type.82
  (14 shorter events, 0.1 us)
Async XLA Ops:
  6.5 323.0 %copy-start = (bf16[8192,128]{1,0:T(8,128)(2,1)S(1)}, bf16[8192,128]{1,0:T(8,128)(2,1)}, u32[]{:S(2)}) copy-start(bf16[8192,128]{1,0:T(8,128)(2,1)} %param.15) | copy-start | bytes 6291460
  28.7 8.3 %copy-start.4 = (s32[32]{0:T(128)S(1)}, s32[32]{0:T(128)}, u32[]{:S(2)}) copy-start(s32[32]{0:T(128)} %param.20) | copy-start | bytes 388
  28.7 8.3 %copy-start.5 = (s32[32]{0:T(128)S(1)}, s32[32]{0:T(128)}, u32[]{:S(2)}) copy-start(s32[32]{0:T(128)} %param.21) | copy-start | bytes 388
  28.7 8.3 %copy-start.6 = (s32[32]{0:T(128)S(1)}, s32[32]{0:T(128)}, u32[]{:S(2)}) copy-start(s32[32]{0:T(128)} %param.19) | copy-start | bytes 388
  28.7 154.3 %all-to-all-start = ((bf16[16,32,8192]{2,1,0:T(8,128)(2,1)}), bf16[16,32,8192]{2,1,0:T(8,128)(2,1)}, u32[]{:S(2)}, u32[]{:S(2)}) async-start(bf16[16,32,8192]{2,1,0:T(8,128)(2,1)} %copy.64), calls=%async_computation | async-start | bytes 16777216 | tf_op jit(solution)/shard_map/all_to_all | solution.py:140
  196.4 101.5 %all-to-all-start.1 = ((bf16[8,32,2,8192]{3,1,2,0:T(8,128)(2,1)}), bf16[8,32,2,8192]{3,1,2,0:T(8,128)(2,1)}, u32[]{:S(2)}, u32[]{:S(2)}) async-start(bf16[8,32,2,8192]{3,1,2,0:T(8,128)(2,1)} %stack.2), calls=%async_computation.1 | async-start | bytes 16777216 | tf_op jit(solution)/shard_map/all_to_all | solution.py:36
  204.0 267.5 %reduce-scatter.2.cloned.1.call-start = ((), (), s32[]{:S(2)}) async-start(), calls=%async_computation.4 | async-start | bytes 9437184 | tf_op jit(solution)/shard_map/reduce_scatter | solution.py:157
  297.8 7.7 %copy-start.3 = (bf16[8192,128]{1,0:T(8,128)(2,1)S(1)}, bf16[8192,128]{1,0:T(8,128)(2,1)}, u32[]{:S(2)}) copy-start(bf16[8192,128]{1,0:T(8,128)(2,1)} %param.14) | copy-start | bytes 6291460
  305.6 7.1 %copy-start.2 = (bf16[8,32,2,8192]{3,1,0,2:T(8,128)(2,1)S(1)}, bf16[8,32,2,8192]{3,1,0,2:T(8,128)(2,1)}, u32[]{:S(2)}) copy-start(bf16[8,32,2,8192]{3,1,0,2:T(8,128)(2,1)} %copy.67) | copy-start | bytes 25165828
  312.6 7.2 %copy-start.7 = (bf16[2,2048,128]{2,1,0:T(8,128)(2,1)S(1)}, bf16[2,2048,128]{2,1,0:T(8,128)(2,1)}, u32[]{:S(2)}) copy-start(bf16[2,2048,128]{2,1,0:T(8,128)(2,1)} %param.17) | copy-start | bytes 3145732
  411.5 62.6 %copy-start.1 = (bf16[8192,128]{1,0:T(8,128)(2,1)S(1)}, bf16[8192,128]{1,0:T(8,128)(2,1)}, u32[]{:S(2)}) copy-start(bf16[8192,128]{1,0:T(8,128)(2,1)} %param.15) | copy-start | bytes 6291460
Sparse Core Ops, SparseCore 0:
  421.9 49.6 reduce-scatter.1
